TPU v7x, 32 devices: a whole 2x2x4 slice. The times are simulated.
32 devices in a mesh: clus: 16 (over z, y, x), sub: 2 (over core).
Axes of the slice: x: 2, y: 2, z: 4, core: 2. Of those that a mesh axis runs over, the one named last changes fastest.
Arguments:
- dual_ops: float32 [64, 1536, 1536], P(('clus', 'sub')), may hold values from 0 to 3, as said below
- rigid_modes: float32 [64, 6, 1536], P(('clus', 'sub')), may hold values from -6 to 6
- members: int32 [64, 4, 1536], P(('clus', 'sub')), may hold values from 0 to 6144, as said below
- coarse_inverse: float32 [384, 384], P(('clus', 'sub')), may hold values from -1 to 1
- dual_rhs: float32 [64, 1536, 128], P(('clus', 'sub')), may hold values from -12 to 12
- coarse_rhs: float32 [64, 6, 128], P(('clus', 'sub')), may hold values from -512 to 512
Outputs:
- multipliers: float32 [64, 1536, 128], P(('clus', 'sub'))
- projected: float32 [64, 1536, 128], P(('clus', 'sub'))
Inputs may be any that keep to these rules, and one draw needn't show every extreme that they name: Every slot's group lists the slot itself first (its own position (s % 2) * 1536 + i), holds 1 to 4 slots of different subdomains, and is the same set for every slot in it; the group of every slot i >= 256 is that slot and one slot >= 256 of the other subdomain of the same device (members[s, 2:, i] = EMPTY); exported entries name only slots among the first 256 of a subdomain on devices with o in 0, 1, 2 that exist. Number the exported slots of a device k = 256 j + i for slot i of its j-th subdomain, and let E = 512: those with k < E / 4 are named only by groups of the other device of the same cluster; E / 4 <= k < E / 2 only by the device of cluster c + 1 with the same t; E / 2 <= k < 3 E / 4 only by the device of cluster c - 1 with the same t; 3 E / 4 <= k < 7 E / 8 only by the other device of the same cluster and the devices of cluster c + 1; 7 E / 8 <= k only by the other device of the same cluster and the devices of cluster c - 1. In each dual_ops[s] every row's off-diagonal entries sum in magnitude to less than its diagonal entry.
All inputs are finite; a program needn't handle non-finite values.
Results may differ from a plain program's by a relative error of at most 0.00015.
Values sent between devices are 32-bit elements; how exact they have to be, the bound alone decides.
A program may use at most 128 MiB of HBM per device.

v0:
```python
import jax
import jax.numpy as jnp
from jax import lax
from jax.sharding import PartitionSpec as P

ESUB = 256
ITERS = 2


def shifted(value, axis, steps):
    count = lax.axis_size(axis)
    leading, last = (max(0, -steps), min(count, count - steps))
    return lax.ppermute(value, axis, [(source, source + steps) for source in range(leading, last)])


def pair_product(first_field, second_field):
    return jnp.sum(first_field * second_field, axis=(0, 1))


def square_sum(field):
    return lax.psum(pair_product(field, field), ("clus", "sub"))


def on_device(dual_ops, rigid_modes, members, coarse_inverse, dual_rhs, coarse_rhs):
    sub_count, slot_count, load_cases = dual_rhs.shape
    local_rows = sub_count * slot_count
    export_rows = sub_count * ESUB
    pad_index = local_rows + 6 * export_rows
    quarter = export_rows // 4
    eighth = export_rows // 8
    share_rows = quarter + 4 * eighth
    group_count = members.shape[1]
    tables = jnp.transpose(members, (1, 0, 2)).reshape(group_count, local_rows)
    group_size = jnp.sum((tables < pad_index).astype(jnp.float32), axis=0)[:, None]
    offset = tables - local_rows
    cycle_block = offset // export_rows
    within = offset % export_rows
    inside = (tables >= local_rows) & (tables < pad_index)
    own_half = lax.axis_index("sub")
    neighbour = cycle_block // 2
    source_half = cycle_block % 2
    from_own = source_half == own_half
    above_start = local_rows + quarter + eighth
    pair_start = above_start + quarter + eighth
    shared_base = pair_start + source_half * share_rows
    lower_rows = jnp.where(
        within < 2 * quarter,
        local_rows + within - quarter,
        jnp.where(
            from_own,
            local_rows + quarter + within - 3 * quarter,
            shared_base + quarter + 2 * eighth + within - 3 * quarter,
        ),
    )
    upper_rows = jnp.where(
        within < 3 * quarter,
        above_start + within - 2 * quarter,
        jnp.where(
            from_own,
            above_start + quarter + within - 3 * quarter - eighth,
            shared_base + quarter + 3 * eighth + within - 3 * quarter - eighth,
        ),
    )
    pair_rows = jnp.where(
        within < quarter, shared_base + within, shared_base + quarter + within - 3 * quarter
    )
    remote = jnp.where(neighbour == 0, lower_rows, jnp.where(neighbour == 1, pair_rows, upper_rows))
    empty_at = pair_start + 2 * share_rows
    tables = jnp.where(tables < local_rows, tables, jnp.where(inside, remote, empty_at))
    other_members = tables[1:].reshape(-1)
    empty_row = jnp.zeros((1, load_cases), jnp.float32)

    def jump_part(field):
        flat_field = field.reshape(local_rows, load_cases)
        outgoing = field[:, :ESUB, :].reshape(export_rows, load_cases)
        upward = jnp.concatenate(
            [outgoing[quarter : 2 * quarter], outgoing[3 * quarter : 3 * quarter + eighth]], axis=0
        )
        downward = jnp.concatenate(
            [outgoing[2 * quarter : 3 * quarter], outgoing[3 * quarter + eighth :]], axis=0
        )
        below = shifted(upward, "clus", 1)
        above = shifted(downward, "clus", -1)
        shared = jnp.concatenate(
            [outgoing[:quarter], outgoing[3 * quarter :], below[quarter:], above[quarter:]], axis=0
        )
        gathered = jnp.concatenate(
            [below, above, lax.all_gather(shared, "sub", axis=0, tiled=True)], axis=0
        )
        pool_rows = jnp.concatenate([flat_field, gathered, empty_row], axis=0)
        picked = jnp.take(pool_rows, other_members, axis=0).reshape(
            group_count - 1, local_rows, load_cases
        )
        group_total = flat_field
        for member in range(group_count - 1):
            group_total = group_total + picked[member]
        return (flat_field - group_total / group_size).reshape(field.shape)

    def lift(terms):
        weights = jnp.dot(
            coarse_inverse,
            lax.all_gather(terms, ("clus", "sub"), axis=0, tiled=True),
            precision=lax.Precision.HIGHEST,
            preferred_element_type=jnp.float32,
        )
        weights = weights.reshape(sub_count, rigid_modes.shape[1], load_cases)
        return jump_part(
            jnp.einsum("jkm,jkn->jmn", rigid_modes, weights, precision=lax.Precision.HIGHEST)
        )

    def restrict(field):
        return jnp.einsum(
            "jkm,jmn->jkn", rigid_modes, field, precision=lax.Precision.HIGHEST
        ).reshape(-1, load_cases)

    def project(field):
        return field - lift(restrict(field))

    def blockwise(field):
        return jnp.einsum("jmq,jqn->jmn", dual_ops, field, precision=lax.Precision.HIGHEST)

    multipliers = lift(coarse_rhs.reshape(-1, load_cases))
    residual_now = jump_part(dual_rhs - blockwise(multipliers))
    projected = project(residual_now)
    direction = projected
    norm_now = square_sum(projected)
    for iteration in range(ITERS):
        along = jump_part(blockwise(direction))
        curvature_now = lax.psum(pair_product(direction, along), ("clus", "sub"))
        step_size = (norm_now / curvature_now)[None, None, :]
        multipliers = multipliers + step_size * direction
        residual_now = residual_now - step_size * along
        projected = project(residual_now)
        if iteration + 1 < ITERS:
            norm_next = square_sum(projected)
            direction = projected + (norm_next / norm_now)[None, None, :] * direction
            norm_now = norm_next
    return (multipliers, projected)


def solution(mesh):
    return jax.shard_map(
        on_device,
        mesh=mesh,
        in_specs=(
            P(("clus", "sub"), None, None),
            P(("clus", "sub"), None, None),
            P(("clus", "sub"), None, None),
            P(("clus", "sub"), None),
            P(("clus", "sub"), None, None),
            P(("clus", "sub"), None, None),
        ),
        out_specs=(P(("clus", "sub"), None, None), P(("clus", "sub"), None, None)),
        check_vma=False,
    )
```

profile of v0, /device:TPU:0, one launch (start us, length us, event | category | flops | bytes accessed | tf_op | source)
XLA Modules:
  0.0 818.4 jit_solution(16906384568805584855)
XLA Ops:
  1.4 43.9 %all-gather = f32[32,12,128]{2,1,0:T(8,128)S(1)} all-gather(f32[1,12,128]{2,1,0:T(8,128)S(1)} %reshape.286), channel_id=1, replica_groups=mesh['clus'=16,'sub'=2] {'clus','sub'}, dimensions={0}, use_global_device_ids=true | all-gather | bytes 202752 | tf_op jit(solution)/shard_map/all_gather | solution.py:102
  59.8 30.9 %gather_fusion = f32[9216,128]{1,0:T(8,128)} fusion(f32[4225,128]{1,0:T(8,128)S(1)} %dynamic-update-slice.34, s32[9216]{0:T(1024)S(1)} %fusion.17), kind=kCustom, calls=%fused_computation.clone | custom fusion | bytes 9474048 | tf_op jit(solution)/shard_map/jit(_take)/gather | solution.py:91
  90.8 6.6 broadcast_select_fusion.6
  108.4 23.3 %fusion = f32[2,1536,128]{1,2,0:T(8,128)S(1)} fusion(f32[2,1536,128]{1,2,0:T(8,128)S(1)} %copy-done.24, f32[2,1536,128]{1,2,0:T(8,128)S(1)} %divide_subtract_fusion.3, f32[2,1536,1536]{2,1,0:T(8,128)} %param.8), kind=kOutput, calls=%fused_computation.14 | convolution fusion | flops 7248150528 | bytes 23592960 | tf_op jit(solution)/shard_map/jmq,jqn->jmn/dot_general | solution.py:120
  147.0 30.9 %gather_fusion.1 = f32[9216,128]{1,0:T(8,128)} fusion(f32[4225,128]{1,0:T(8,128)S(1)} %dynamic-update-slice.29, s32[9216]{0:T(1024)S(1)} %fusion.17), kind=kCustom, calls=%fused_computation.1.clone | custom fusion | bytes 9474048 | tf_op jit(solution)/shard_map/jit(_take)/gather | solution.py:91
  178.0 6.6 broadcast_select_fusion.5
  198.0 38.8 %all-gather.1 = f32[32,12,128]{2,1,0:T(8,128)S(1)} all-gather(f32[1,12,128]{2,1,0:T(8,128)S(1)} %reshape.288), channel_id=1, replica_groups=mesh['clus'=16,'sub'=2] {'clus','sub'}, dimensions={0}, use_global_device_ids=true | all-gather | bytes 202752 | tf_op jit(solution)/shard_map/all_gather | solution.py:102
  251.7 30.9 %gather_fusion.2 = f32[9216,128]{1,0:T(8,128)} fusion(f32[4225,128]{1,0:T(8,128)S(1)} %dynamic-update-slice.24, s32[9216]{0:T(1024)S(1)} %fusion.17), kind=kCustom, calls=%fused_computation.2.clone | custom fusion | bytes 9474048 | tf_op jit(solution)/shard_map/jit(_take)/gather | solution.py:91
  282.7 6.6 broadcast_select_fusion.4
  300.6 23.3 %convolution_bitcast_fusion.3 = f32[2,1536,128]{1,2,0:T(8,128)S(1)} fusion(f32[2,1536,128]{1,2,0:T(8,128)S(1)} %subtract_subtract_fusion.2, f32[2,1536,1536]{2,1,0:T(8,128)} %param.8), kind=kOutput, calls=%fused_computation.10 | convolution fusion | flops 7247757312 | bytes 22020096 | tf_op jit(solution)/shard_map/jmq,jqn->jmn/dot_general | solution.py:120
  338.1 30.9 %gather_fusion.3 = f32[9216,128]{1,0:T(8,128)} fusion(f32[4225,128]{1,0:T(8,128)S(1)} %dynamic-update-slice.19, s32[9216]{0:T(1024)S(1)} %fusion.17), kind=kCustom, calls=%fused_computation.3.clone | custom fusion | bytes 9474048 | tf_op jit(solution)/shard_map/jit(_take)/gather | solution.py:91
  369.0 6.6 broadcast_select_fusion.3
  388.1 37.2 %all-reduce = (f32[128]{0:T(128)S(1)}, f32[128]{0:T(128)S(1)}) all-reduce(f32[128]{0:T(128)S(1)} %get-tuple-element.10, f32[128]{0:T(128)S(1)} %get-tuple-element.9), channel_id=1, replica_groups=mesh['clus'=16,'sub'=2] {'clus','sub'}, use_global_device_ids=true, to_apply=%region_2.4 | all-reduce | flops 256 | bytes 2048 | tf_op jit(solution)/shard_map/psum | solution.py:21
  429.7 41.2 %all-gather.2 = f32[32,12,128]{2,1,0:T(8,128)S(1)} all-gather(f32[1,12,128]{2,1,0:T(8,128)S(1)} %reshape.290), channel_id=1, replica_groups=mesh['clus'=16,'sub'=2] {'clus','sub'}, dimensions={0}, use_global_device_ids=true | all-gather | bytes 202752 | tf_op jit(solution)/shard_map/all_gather | solution.py:102
  485.0 30.9 %gather_fusion.4 = f32[9216,128]{1,0:T(8,128)} fusion(f32[4225,128]{1,0:T(8,128)S(1)} %dynamic-update-slice.14, s32[9216]{0:T(1024)S(1)} %fusion.17), kind=kCustom, calls=%fused_computation.4.clone | custom fusion | bytes 9474048 | tf_op jit(solution)/shard_map/jit(_take)/gather | solution.py:91
  515.9 6.6 broadcast_select_fusion.2
  535.2 37.0 %psum.30 = f32[128]{0:T(128)S(1)} all-reduce(f32[128]{0:T(128)S(1)} %get-tuple-element.15), channel_id=1, replica_groups=mesh['clus'=16,'sub'=2] {'clus','sub'}, use_global_device_ids=true, to_apply=%region_6.8 | all-reduce | flops 128 | bytes 1024 | tf_op jit(solution)/shard_map/psum | solution.py:21
  572.2 22.5 %convolution_bitcast_fusion.1 = f32[2,1536,128]{1,2,0:T(8,128)S(1)} fusion(f32[2,1536,1536]{2,1,0:T(8,128)} %param.8, f32[2,1536,128]{1,2,0:T(8,128)} %get-tuple-element.16, f32[2,1536,128]{1,2,0:T(8,128)S(1)} %copy-done.3, f32[128]{0:T(128)S(1)} %div.94), kind=kOutput, calls=%fused_computation.8 | convolution fusion | flops 7248543744 | bytes 23593472 | tf_op jit(solution)/shard_map/jmq,jqn->jmn/dot_general | solution.py:120
  609.5 30.9 %gather_fusion.5 = f32[9216,128]{1,0:T(8,128)} fusion(f32[4225,128]{1,0:T(8,128)S(1)} %dynamic-update-slice.9, s32[9216]{0:T(1024)S(1)} %fusion.17), kind=kCustom, calls=%fused_computation.5.clone | custom fusion | bytes 9474048 | tf_op jit(solution)/shard_map/jit(_take)/gather | solution.py:91
  640.5 6.6 broadcast_select_fusion.1
  660.3 41.6 %psum.31 = f32[128]{0:T(128)S(1)} all-reduce(f32[128]{0:T(128)S(1)} %get-tuple-element.13), channel_id=1, replica_groups=mesh['clus'=16,'sub'=2] {'clus','sub'}, use_global_device_ids=true, to_apply=%region_8.10 | all-reduce | flops 128 | bytes 1024 | tf_op jit(solution)/shard_map/psum | solution.py:129
  705.0 41.2 %all-gather.3 = f32[32,12,128]{2,1,0:T(8,128)S(1)} all-gather(f32[1,12,128]{2,1,0:T(8,128)S(1)} %reshape.292), channel_id=1, replica_groups=mesh['clus'=16,'sub'=2] {'clus','sub'}, dimensions={0}, use_global_device_ids=true | all-gather | bytes 202752 | tf_op jit(solution)/shard_map/all_gather | solution.py:102
  760.3 30.9 %gather_fusion.6 = f32[9216,128]{1,0:T(8,128)} fusion(f32[4225,128]{1,0:T(8,128)S(1)} %dynamic-update-slice.4, s32[9216]{0:T(1024)S(1)} %fusion.17), kind=kCustom, calls=%fused_computation.6.clone | custom fusion | bytes 9474048 | tf_op jit(solution)/shard_map/jit(_take)/gather | solution.py:91
  805.9 7.6 subtract_subtract_fusion
  (272 shorter events, 202.5 us)
Async XLA Ops:
  0.6 45.7 %copy-start = (f32[2,6,1536]{2,0,1:T(2,128)S(1)}, f32[2,6,1536]{2,0,1:T(2,128)}, u32[]{:S(2)}) copy-start(f32[2,6,1536]{2,0,1:T(2,128)} %param.9) | copy-start | bytes 221188
  46.3 4.3 copy-start.26
  47.8 3.4 copy-start.19
  48.0 9.4 %collective-permute-start = (f32[192,128]{1,0:T(8,128)S(1)}, f32[192,128]{1,0:T(8,128)S(1)}, u32[]{:S(2)}, u32[]{:S(2)}) collective-permute-start(f32[192,128]{1,0:T(8,128)S(1)} %pad_maximum_fusion.7), channel_id=1, source_target_pairs={{0,2},{2,4},{4,6},{6,8},{8,10},{10,12},{12,14},{14,16},{16,18},{18... | collective-permute-start | bytes 294920 | tf_op jit(solution)/shard_map/ppermute | solution.py:13
  49.3 8.1 collective-permute-start.1
  108.4 23.3 %copy-start.23 = (f32[2,1536,128]{1,2,0:T(8,128)}, f32[2,1536,128]{1,2,0:T(8,128)S(1)}, u32[]{:S(2)}) copy-start(f32[2,1536,128]{1,2,0:T(8,128)S(1)} %divide_subtract_fusion.3) | copy-start | bytes 4718596
  133.5 7.4 collective-permute-start.2
  138.1 6.5 collective-permute-start.3
  196.6 40.2 %copy-start.27 = (f32[12,384]{1,0:T(8,128)S(1)}, f32[12,384]{1,0:T(8,128)}, u32[]{:S(2)}) copy-start(f32[12,384]{1,0:T(8,128)} %param.11) | copy-start | bytes 55300
  240.4 6.8 collective-permute-start.4
  242.6 6.7 collective-permute-start.5
  300.5 23.3 %copy-start.1 = (f32[2,1536,128]{1,2,0:T(8,128)}, f32[2,1536,128]{1,2,0:T(8,128)S(1)}, u32[]{:S(2)}) copy-start(f32[2,1536,128]{1,2,0:T(8,128)S(1)} %subtract_subtract_fusion.2) | copy-start | bytes 4718596
  325.8 7.5 collective-permute-start.6
  328.9 6.5 collective-permute-start.7
  383.5 41.9 %copy-start.12 = (f32[2,1536,128]{1,2,0:T(8,128)S(1)}, f32[2,1536,128]{1,2,0:T(8,128)}, u32[]{:S(2)}) copy-start(f32[2,1536,128]{1,2,0:T(8,128)} %copy-done.10) | copy-start | bytes 4718596
  474.5 6.2 collective-permute-start.8
  475.8 6.9 collective-permute-start.9
  530.3 41.9 %copy-start.3 = (f32[2,1536,128]{1,2,0:T(8,128)S(1)}, f32[2,1536,128]{1,2,0:T(8,128)}, u32[]{:S(2)}) copy-start(f32[2,1536,128]{1,2,0:T(8,128)} %copy-done.1) | copy-start | bytes 4718596
  596.6 7.0 collective-permute-start.10
  600.8 6.5 collective-permute-start.11
  655.0 46.9 %copy-start.8 = (f32[2,1536,128]{1,2,0:T(8,128)S(1)}, f32[2,1536,128]{1,2,0:T(8,128)}, u32[]{:S(2)}) copy-start(f32[2,1536,128]{1,2,0:T(8,128)} %copy-done.6) | copy-start | bytes 4718596
  749.8 6.2 collective-permute-start.12
  751.1 6.9 collective-permute-start.13
  802.7 3.2 copy-start.9
  (18 other events, 37.6 us)
where the time goes:
time: 824 us; the launch traced here: 818 us
  local copies, waits for them, and re-layouts  308 us (37%)
  blocking collectives  295 us (36%)
  matrix products  82.4 us (10%)
  other arithmetic  80.8 us (10%)
  starting transfers between devices  26.9 us (3%)
  waiting for transfers between devices  23.1 us (3%)
    gather x7, local copies, waits for them, and re-layouts, jump_part(): jnp.take(pool_rows, other_members, axis=0)  217 us
    all_gather x4, blocking collectives, lift(): lax.all_gather(terms, ('clus', 'sub'), axis=0, tiled=True)  165 us
    psum x2, blocking collectives, square_sum(): return lax.psum(pair_product(field, field), ('clus', 'sub'))  74.2 us
    dot_general x3, matrix products, blockwise(): jnp.einsum('jmq,jqn->jmn', dual_ops, field, precision=lax.Precision.HIGHEST)  69.1 us
    select_n x7, other arithmetic, jump_part(): jnp.take(pool_rows, other_members, axis=0)  46.4 us
    squeeze x21, local copies, waits for them, and re-layouts, jump_part(): group_total = group_total + picked[member]  44.6 us
    psum x1, blocking collectives, on_device(): curvature_now = lax.psum(pair_product(direction, along), ('clus', 'sub'))  41.6 us
    ppermute x14, starting transfers between devices, shifted(): lax.ppermute(value, axis, [(source, source + steps) for source in range(l...  26.9 us
  transfers between devices with their start and end apart: 14, of which 10 were waited for; matrix products, arithmetic and copies ran while one was open for 2% of the time, Pallas kernels for 0%

commit v1 on v0

--- a/solution.py
+++ b/solution.py
@@ -5,6 +5,11 @@
 
 ESUB = 256
 ITERS = 2
+
+
+def axis_by_axis(array, inner_axis, outer_axis):
+    inner = lax.psum(array, inner_axis)
+    return lax.psum(inner, outer_axis)
 
 
 def shifted(value, axis, steps):
@@ -18,7 +23,7 @@
 
 
 def square_sum(field):
-    return lax.psum(pair_product(field, field), ("clus", "sub"))
+    return axis_by_axis(pair_product(field, field), "sub", "clus")
 
 
 def on_device(dual_ops, rigid_modes, members, coarse_inverse, dual_rhs, coarse_rhs):

time: 824 us -> 863 us (1.047)
  blocking collectives: 295 us -> 333 us
    psum x1 -> x2, blocking collectives: 41.6 us -> 74 us  [on_device(): curvature_now = lax.psum(pair_product(direction, along), ('clus', 'sub'))]
    psum x2 -> x4, blocking collectives: 74.2 us -> 83.6 us  [the longest x2 78.7 us: axis_by_axis(): return lax.psum(inner, outer_axis)]
  transfers between devices with their start and end apart: 14 -> 14, of which waited for: 10 -> 11; matrix products, arithmetic and copies ran while one was open for 2% -> 2% of each run, Pallas kernels for 0% -> 0%
where the time goes in v1:
time: 863 us; the launch traced here: 858 us
  blocking collectives  333 us (39%)
  local copies, waits for them, and re-layouts  308 us (36%)
  matrix products  82.4 us (10%)
  other arithmetic  80.7 us (9%)
  starting transfers between devices  28.1 us (3%)
  waiting for transfers between devices  22.9 us (3%)
    gather x7, local copies, waits for them, and re-layouts, jump_part(): jnp.take(pool_rows, other_members, axis=0)  217 us
    all_gather x4, blocking collectives, lift(): lax.all_gather(terms, ('clus', 'sub'), axis=0, tiled=True)  161 us
    psum x2, blocking collectives, axis_by_axis(): return lax.psum(inner, outer_axis)  78.7 us
    psum x2, blocking collectives, on_device(): curvature_now = lax.psum(pair_product(direction, along), ('clus', 'sub'))  74 us
    dot_general x3, matrix products, blockwise(): jnp.einsum('jmq,jqn->jmn', dual_ops, field, precision=lax.Precision.HIGHEST)  69.1 us
    select_n x7, other arithmetic, jump_part(): jnp.take(pool_rows, other_members, axis=0)  46.4 us
    squeeze x21, local copies, waits for them, and re-layouts, jump_part(): group_total = group_total + picked[member]  44.5 us
    ppermute x14, starting transfers between devices, shifted(): lax.ppermute(value, axis, [(source, source + steps) for source in range(l...  28.1 us
  transfers between devices with their start and end apart: 14, of which 11 were waited for; matrix products, arithmetic and copies ran while one was open for 2% of the time, Pallas kernels for 0%

profile of v1, /device:TPU:0, one launch (start us, length us, event | category | flops | bytes accessed | tf_op | source)
XLA Modules:
  0.0 857.6 jit_solution(184340779485826565)
XLA Ops:
  1.4 43.9 %all-gather = f32[32,12,128]{2,1,0:T(8,128)S(1)} all-gather(f32[1,12,128]{2,1,0:T(8,128)S(1)} %reshape.286), channel_id=1, replica_groups=mesh['clus'=16,'sub'=2] {'clus','sub'}, dimensions={0}, use_global_device_ids=true | all-gather | bytes 202752 | tf_op jit(solution)/shard_map/all_gather | solution.py:107
  59.8 31.0 %gather_fusion = f32[9216,128]{1,0:T(8,128)} fusion(f32[4225,128]{1,0:T(8,128)S(1)} %dynamic-update-slice.34, s32[9216]{0:T(1024)S(1)} %fusion.17), kind=kCustom, calls=%fused_computation.clone | custom fusion | bytes 9474048 | tf_op jit(solution)/shard_map/jit(_take)/gather | solution.py:96
  90.9 6.6 broadcast_select_fusion.6
  108.4 23.3 %fusion = f32[2,1536,128]{1,2,0:T(8,128)S(1)} fusion(f32[2,1536,128]{1,2,0:T(8,128)S(1)} %copy-done.24, f32[2,1536,128]{1,2,0:T(8,128)S(1)} %divide_subtract_fusion.3, f32[2,1536,1536]{2,1,0:T(8,128)} %param.8), kind=kOutput, calls=%fused_computation.14 | convolution fusion | flops 7248150528 | bytes 23592960 | tf_op jit(solution)/shard_map/jmq,jqn->jmn/dot_general | solution.py:125
  147.1 31.0 %gather_fusion.1 = f32[9216,128]{1,0:T(8,128)} fusion(f32[4225,128]{1,0:T(8,128)S(1)} %dynamic-update-slice.29, s32[9216]{0:T(1024)S(1)} %fusion.17), kind=kCustom, calls=%fused_computation.1.clone | custom fusion | bytes 9474048 | tf_op jit(solution)/shard_map/jit(_take)/gather | solution.py:96
  178.1 6.6 broadcast_select_fusion.5
  198.1 38.8 %all-gather.1 = f32[32,12,128]{2,1,0:T(8,128)S(1)} all-gather(f32[1,12,128]{2,1,0:T(8,128)S(1)} %reshape.288), channel_id=1, replica_groups=mesh['clus'=16,'sub'=2] {'clus','sub'}, dimensions={0}, use_global_device_ids=true | all-gather | bytes 202752 | tf_op jit(solution)/shard_map/all_gather | solution.py:107
  251.8 31.0 %gather_fusion.2 = f32[9216,128]{1,0:T(8,128)} fusion(f32[4225,128]{1,0:T(8,128)S(1)} %dynamic-update-slice.24, s32[9216]{0:T(1024)S(1)} %fusion.17), kind=kCustom, calls=%fused_computation.2.clone | custom fusion | bytes 9474048 | tf_op jit(solution)/shard_map/jit(_take)/gather | solution.py:96
  282.9 6.6 broadcast_select_fusion.4
  300.7 23.3 %convolution_bitcast_fusion.3 = f32[2,1536,128]{1,2,0:T(8,128)S(1)} fusion(f32[2,1536,128]{1,2,0:T(8,128)S(1)} %subtract_subtract_fusion.2, f32[2,1536,1536]{2,1,0:T(8,128)} %param.8), kind=kOutput, calls=%fused_computation.10 | convolution fusion | flops 7247757312 | bytes 22020096 | tf_op jit(solution)/shard_map/jmq,jqn->jmn/dot_general | solution.py:125
  338.2 31.0 %gather_fusion.3 = f32[9216,128]{1,0:T(8,128)} fusion(f32[4225,128]{1,0:T(8,128)S(1)} %dynamic-update-slice.19, s32[9216]{0:T(1024)S(1)} %fusion.17), kind=kCustom, calls=%fused_computation.3.clone | custom fusion | bytes 9474048 | tf_op jit(solution)/shard_map/jit(_take)/gather | solution.py:96
  369.3 6.6 broadcast_select_fusion.3
  388.3 37.2 %psum.44 = f32[128]{0:T(128)S(1)} all-reduce(f32[128]{0:T(128)S(1)} %get-tuple-element.9), channel_id=1, replica_groups=mesh['clus'=16,'sub'=2] {'clus','sub'}, use_global_device_ids=true, to_apply=%region_5.7 | all-reduce | flops 128 | bytes 1024 | tf_op jit(solution)/shard_map/psum | solution.py:134
  428.0 40.8 %psum.43 = f32[128]{0:T(128)S(1)} all-reduce(f32[128]{0:T(128)S(1)} %psum.42), channel_id=1, replica_groups=mesh['clus'=16,'sub'=2] {'clus'}, use_global_device_ids=true, to_apply=%region_3.5 | all-reduce | flops 128 | bytes 1024 | tf_op jit(solution)/shard_map/psum | solution.py:12
  473.1 37.0 %all-gather.2 = f32[32,12,128]{2,1,0:T(8,128)S(1)} all-gather(f32[1,12,128]{2,1,0:T(8,128)S(1)} %reshape.290), channel_id=1, replica_groups=mesh['clus'=16,'sub'=2] {'clus','sub'}, dimensions={0}, use_global_device_ids=true | all-gather | bytes 202752 | tf_op jit(solution)/shard_map/all_gather | solution.py:107
  526.5 31.0 %gather_fusion.4 = f32[9216,128]{1,0:T(8,128)} fusion(f32[4225,128]{1,0:T(8,128)S(1)} %dynamic-update-slice.14, s32[9216]{0:T(1024)S(1)} %fusion.17), kind=kCustom, calls=%fused_computation.4.clone | custom fusion | bytes 9474048 | tf_op jit(solution)/shard_map/jit(_take)/gather | solution.py:96
  557.5 6.6 broadcast_select_fusion.2
  579.2 37.9 %psum.46 = f32[128]{0:T(128)S(1)} all-reduce(f32[128]{0:T(128)S(1)} %psum.45), channel_id=1, replica_groups=mesh['clus'=16,'sub'=2] {'clus'}, use_global_device_ids=true, to_apply=%region_8.10 | all-reduce | flops 128 | bytes 1024 | tf_op jit(solution)/shard_map/psum | solution.py:12
  617.1 22.5 %convolution_bitcast_fusion.1 = f32[2,1536,128]{1,2,0:T(8,128)S(1)} fusion(f32[2,1536,1536]{2,1,0:T(8,128)} %param.8, f32[2,1536,128]{1,2,0:T(8,128)} %get-tuple-element.14, f32[2,1536,128]{1,2,0:T(8,128)S(1)} %copy-done.3, f32[128]{0:T(128)S(1)} %div.94), kind=kOutput, calls=%fused_computation.8 | convolution fusion | flops 7248543744 | bytes 23593472 | tf_op jit(solution)/shard_map/jmq,jqn->jmn/dot_general | solution.py:125
  653.0 31.0 %gather_fusion.5 = f32[9216,128]{1,0:T(8,128)} fusion(f32[4225,128]{1,0:T(8,128)S(1)} %dynamic-update-slice.9, s32[9216]{0:T(1024)S(1)} %fusion.17), kind=kCustom, calls=%fused_computation.5.clone | custom fusion | bytes 9474048 | tf_op jit(solution)/shard_map/jit(_take)/gather | solution.py:96
  703.8 36.8 %psum.47 = f32[128]{0:T(128)S(1)} all-reduce(f32[128]{0:T(128)S(1)} %get-tuple-element.11), channel_id=1, replica_groups=mesh['clus'=16,'sub'=2] {'clus','sub'}, use_global_device_ids=true, to_apply=%region_10.12 | all-reduce | flops 128 | bytes 1024 | tf_op jit(solution)/shard_map/psum | solution.py:134
  743.7 41.6 %all-gather.3 = f32[32,12,128]{2,1,0:T(8,128)S(1)} all-gather(f32[1,12,128]{2,1,0:T(8,128)S(1)} %reshape.292), channel_id=1, replica_groups=mesh['clus'=16,'sub'=2] {'clus','sub'}, dimensions={0}, use_global_device_ids=true | all-gather | bytes 202752 | tf_op jit(solution)/shard_map/all_gather | solution.py:107
  799.4 31.0 %gather_fusion.6 = f32[9216,128]{1,0:T(8,128)} fusion(f32[4225,128]{1,0:T(8,128)S(1)} %dynamic-update-slice.4, s32[9216]{0:T(1024)S(1)} %fusion.17), kind=kCustom, calls=%fused_computation.6.clone | custom fusion | bytes 9474048 | tf_op jit(solution)/shard_map/jit(_take)/gather | solution.py:96
  845.0 7.6 subtract_subtract_fusion
  (275 shorter events, 214.7 us)
Async XLA Ops:
  0.6 45.7 %copy-start = (f32[2,6,1536]{2,0,1:T(2,128)S(1)}, f32[2,6,1536]{2,0,1:T(2,128)}, u32[]{:S(2)}) copy-start(f32[2,6,1536]{2,0,1:T(2,128)} %param.9) | copy-start | bytes 221188
  46.3 4.3 copy-start.26
  47.8 3.4 copy-start.19
  48.0 9.4 %collective-permute-start = (f32[192,128]{1,0:T(8,128)S(1)}, f32[192,128]{1,0:T(8,128)S(1)}, u32[]{:S(2)}, u32[]{:S(2)}) collective-permute-start(f32[192,128]{1,0:T(8,128)S(1)} %pad_maximum_fusion.7), channel_id=1, source_target_pairs={{0,2},{2,4},{4,6},{6,8},{8,10},{10,12},{12,14},{14,16},{16,18},{18... | collective-permute-start | bytes 294920 | tf_op jit(solution)/shard_map/ppermute | solution.py:18
  49.3 8.1 collective-permute-start.1
  108.4 23.3 %copy-start.23 = (f32[2,1536,128]{1,2,0:T(8,128)}, f32[2,1536,128]{1,2,0:T(8,128)S(1)}, u32[]{:S(2)}) copy-start(f32[2,1536,128]{1,2,0:T(8,128)S(1)} %divide_subtract_fusion.3) | copy-start | bytes 4718596
  133.6 7.4 collective-permute-start.2
  138.1 6.5 collective-permute-start.3
  196.7 40.2 %copy-start.27 = (f32[12,384]{1,0:T(8,128)S(1)}, f32[12,384]{1,0:T(8,128)}, u32[]{:S(2)}) copy-start(f32[12,384]{1,0:T(8,128)} %param.11) | copy-start | bytes 55300
  240.5 6.8 collective-permute-start.4
  242.7 6.7 collective-permute-start.5
  300.7 23.3 %copy-start.1 = (f32[2,1536,128]{1,2,0:T(8,128)}, f32[2,1536,128]{1,2,0:T(8,128)S(1)}, u32[]{:S(2)}) copy-start(f32[2,1536,128]{1,2,0:T(8,128)S(1)} %subtract_subtract_fusion.2) | copy-start | bytes 4718596
  325.9 7.5 collective-permute-start.6
  329.1 6.5 collective-permute-start.7
  383.7 85.1 %copy-start.12 = (f32[2,1536,128]{1,2,0:T(8,128)S(1)}, f32[2,1536,128]{1,2,0:T(8,128)}, u32[]{:S(2)}) copy-start(f32[2,1536,128]{1,2,0:T(8,128)} %copy-done.10) | copy-start | bytes 4718596
  513.7 8.5 collective-permute-start.8
  517.7 6.7 collective-permute-start.9
  571.9 45.2 %copy-start.3 = (f32[2,1536,128]{1,2,0:T(8,128)S(1)}, f32[2,1536,128]{1,2,0:T(8,128)}, u32[]{:S(2)}) copy-start(f32[2,1536,128]{1,2,0:T(8,128)} %copy-done.1) | copy-start | bytes 4718596
  641.5 5.9 collective-permute-start.10
  644.3 6.5 collective-permute-start.11
  698.5 42.1 %copy-start.8 = (f32[2,1536,128]{1,2,0:T(8,128)S(1)}, f32[2,1536,128]{1,2,0:T(8,128)}, u32[]{:S(2)}) copy-start(f32[2,1536,128]{1,2,0:T(8,128)} %copy-done.6) | copy-start | bytes 4718596
  788.9 6.2 collective-permute-start.12
  790.2 6.9 collective-permute-start.13
  841.8 3.2 copy-start.9
  (18 other events, 37.6 us)
